TPU v7x, 32 devices: a whole 2x2x4 slice. The times are simulated.
32 devices in a mesh: day: 2 (over x), row: 16 (over z, y, core).
Axes of the slice: x: 2, y: 2, z: 4, core: 2. Of those that a mesh axis runs over, the one named last changes fastest.
Arguments:
- spectra: bfloat16 [4096, 2, 2, 4096], P(('day', 'row')), parts along dimension 0, may hold values from -110 to 110
- pair_channels: int32 [64, 128, 2], P('row'), may hold values from 0 to 2047, as said below
- pair_live: int32 [64, 128], P('row'), may hold values from 0 to 1, as said below
Outputs:
- correlations: float32 [128, 128, 512], P(('day', 'row')), parts along dimension 0
There are 2 independent parts, one for each index of `day`. A program takes and returns all parts, laid end to end along the dimension named above; an argument that names none is the same for every part. Nothing has to cross between parts.
Inputs may be any that keep to these rules, and one draw needn't show every extreme that they name: `pair_channels`: pair slots of device i of row are tiles i * 4 to (i + 1) * 4 - 1; their first channels are that device's own channels i * 128 to (i + 1) * 128 - 1, and their second channels lie within 128 channels of the first; distances of exactly 128 occur on both sides. `pair_live`: in each device's pair slots (tile by tile, pair by pair) the live slots come first and the padding after; every device has 128 live slots or more, and one device's slots are all live.
All inputs are finite; a program needn't handle non-finite values.
Results may differ from a plain program's by a relative error of at most 0.003.
Values may be sent and summed in bfloat16 or wider, within the bound.
A program may use at most 192 MiB of HBM per device.

v0:
```python
import math

import jax
import jax.numpy as jnp
from jax import lax
from jax.sharding import PartitionSpec as P

WIN = 2
FREQ = 4096
BAND = 64
LAGS = 512
HALO = 128


def padded(block, sides, width):
    for axis, dim in sides:
        count = lax.axis_size(axis)
        forward = [(i, i + 1) for i in range(count - 1)]
        backward = [(target, source) for source, target in forward]
        low = lax.ppermute(
            lax.slice_in_dim(block, block.shape[dim] - width, None, axis=dim), axis, forward
        )
        high = lax.ppermute(lax.slice_in_dim(block, 0, width, axis=dim), axis, backward)
        block = jnp.concatenate([low, block, high], axis=dim)
    return block


def build_table(bin_total, lag_total):
    bin_index = jnp.arange(bin_total, dtype=jnp.int32)[:, None]
    shifts = jnp.arange(lag_total, dtype=jnp.int32)[None, :] - lag_total // 2
    phase_int = jnp.mod(bin_index * shifts, 2 * bin_total)
    angle_rad = phase_int.astype(jnp.float32) * (math.pi / bin_total)
    return jnp.concatenate([jnp.cos(angle_rad), -jnp.sin(angle_rad)], axis=0).astype(jnp.bfloat16)


def whiten(raw_rows, common):
    removed = raw_rows.astype(jnp.float32) - common[None]
    magnitude = jnp.sqrt(removed[:, :, 0] ** 2 + removed[:, :, 1] ** 2)
    row_count, window_count, bin_count = magnitude.shape
    banded = magnitude.reshape(row_count, window_count, bin_count // BAND, BAND)
    band_level = jnp.mean(banded, axis=3, keepdims=True) + 1e-06
    scaled = (
        removed.reshape(row_count, window_count, 2, bin_count // BAND, BAND)
        / band_level[:, :, None]
    )
    return scaled.reshape(raw_rows.shape).astype(jnp.bfloat16)


def cross_rows(first_rows, second_rows):
    first_f32 = first_rows.astype(jnp.float32)
    second_f32 = second_rows.astype(jnp.float32)
    real_part = jnp.sum(
        first_f32[:, :, 0] * second_f32[:, :, 0] + first_f32[:, :, 1] * second_f32[:, :, 1], axis=1
    )
    imag_part = jnp.sum(
        first_f32[:, :, 1] * second_f32[:, :, 0] - first_f32[:, :, 0] * second_f32[:, :, 1], axis=1
    )
    return jnp.concatenate([real_part, imag_part], axis=1).astype(jnp.bfloat16)


def body(spectra, pair_channels, pair_live):
    own_rows = spectra.shape[0]
    channels = own_rows * lax.axis_size("row")
    first_row = lax.axis_index("row") * own_rows - HALO
    local_sum = jnp.sum(spectra, axis=0, dtype=jnp.float32)
    common = lax.psum(local_sum, "row") / channels
    raw_band = padded(spectra, (("row", 0),), HALO)
    band_rows = whiten(raw_band, common)
    lag_matrix = build_table(FREQ, LAGS)
    norm_factor = 1.0 / math.sqrt(FREQ * WIN)
    tile_count = pair_channels.shape[0]
    tile_pairs = pair_channels.shape[1]
    group_count = tile_count // 4
    group_rows = 4 * tile_pairs
    pair_index = (pair_channels - first_row).reshape(group_count, group_rows, 2)
    weights = pair_live.astype(jnp.float32).reshape(group_count, group_rows)

    def correlate(index_rows, weight_rows):
        products = cross_rows(band_rows[index_rows[:, 0]], band_rows[index_rows[:, 1]])
        summed = jnp.dot(products, lag_matrix, preferred_element_type=jnp.float32)
        return summed * norm_factor * weight_rows[:, None]

    def one_group(operands):
        index_rows, weight_rows = operands
        outcome = correlate(index_rows, weight_rows)
        return outcome

    result = lax.map(one_group, (pair_index, weights))
    return result.reshape(tile_count, tile_pairs, LAGS)


def solution(mesh):
    placed = (P(("day", "row"), None, None, None), P("row", None, None), P("row", None))
    return jax.shard_map(
        body, mesh=mesh, in_specs=placed, out_specs=P(("day", "row"), None, None), check_vma=False
    )
```

profile of v0, /device:TPU:7, one launch (start us, length us, event | category | flops | bytes accessed | tf_op | source)
XLA Modules:
  0.0 492.2 jit_solution(6996535282205614045)
XLA Ops:
  6.5 0.0 copy-start.1
  6.5 0.0 copy-start.2
  6.5 0.0 all-reduce.2.cloned.1.call-start
  6.5 7.1 %copy.11 = bf16[128,2,2,4096]{3,0,2,1:T(8,128)(2,1)} copy(bf16[128,2,2,4096]{3,2,1,0:T(2,128)(2,1)} %param.3) | data formatting | bytes 8388608 | tf_op args[0]
  13.6 3.7 collective-permute-start
  17.3 1.9 collective-permute-start.1
  19.3 6.4 %convert_reduce_fusion = f32[2,2,4096]{2,1,0:T(2,128)} fusion(bf16[128,2,2,4096]{3,2,1,0:T(2,128)(2,1)} %param.3), kind=kLoop, calls=%fused_computation.27 | loop fusion | flops 4177920 | bytes 4259840 | tf_op jit(solution)/shard_map/reduce_sum | solution.py:65
  25.6 0.0 all-reduce.2.cloned.1.call-update
  25.7 0.0 copy-done.1
  25.7 0.0 copy-done.2
  25.8 35.2 %cosine_convert_fusion = (bf16[4096,512]{1,0:T(8,128)(2,1)}, bf16[4096,512]{1,0:T(8,128)(2,1)}) fusion(s32[512]{0:T(512)S(1)} %iota_add_fusion), kind=kLoop, calls=%fused_computation.24 | loop fusion | flops 35651584 | bytes 8390656 | tf_op jit(solution)/shard_map/convert
  61.0 82.0 %all-reduce.2.cloned.1.call-done = f32[2,2,4096]{2,1,0:T(2,128)} async-done(((f32[2,2,4096]{2,1,0:T(2,128)}), f32[2,2,4096]{2,1,0:T(2,128)}) %all-reduce.2.cloned.1.call-update) | async-done | bytes 65552 | tf_op jit(solution)/shard_map/psum | solution.py:66
  143.0 0.9 broadcast_multiply_fusion
  143.9 0.0 collective-permute-done
  143.9 0.0 collective-permute-done.1
  143.9 7.4 %convert_subtract_fusion = f32[384,2,2,4096]{3,0,2,1:T(8,128)S(1)} fusion(bf16[128,2,2,4096]{3,0,2,1:T(8,128)(2,1)} %collective-permute-done.1, bf16[128,2,2,4096]{3,0,2,1:T(8,128)(2,1)} %copy.11, bf16[128,2,2,4096]{3,0,2,1:T(8,128)(2,1)} %collective-permute-done, f32[2,2,4096]{2,1,0:T(2,128)S(1)} %broadcast_multiply_fusion), kind=kLoop, calls=%fused_computation.3 | loop fusion | flops 44040192 | bytes 37814272 | tf_op jit(solution)/shard_map/sub | solution.py:37
  151.4 6.7 %fusion.1 = f32[384,2,1,4096]{3,0,2,1:T(8,128)} fusion(f32[384,2,2,4096]{3,0,2,1:T(8,128)S(1)} %convert_subtract_fusion), kind=kLoop, calls=%fused_computation.8 | loop fusion | flops 9437184 | bytes 37748736 | tf_op jit(solution)/shard_map/sqrt | solution.py:38
  158.1 12.6 %copy.14 = f32[384,2,1,4096]{0,3,1,2:T(8,128)} copy(f32[384,2,1,4096]{3,0,2,1:T(8,128)} %fusion.1) | data formatting | bytes 25165824 | tf_op jit(solution)/shard_map/sqrt | solution.py:38
  170.7 6.4 %reduce_sum.39 = f32[384,2,64]{0,2,1:T(8,128)S(1)} reduce(f32[384,2,64,64]{0,3,2,1:T(8,128)} %bitcast.9, f32[]{:T(128)} %constant.25.clone.1), dimensions={3}, to_apply=%region_2.0 | reduce | flops 3096576 | bytes 12779524 | tf_op jit(solution)/shard_map/reduce_sum | solution.py:41
  177.1 5.3 %div.29 = f32[384,2,64,64]{0,3,2,1:T(8,128)} broadcast(f32[384,2,64]{0,2,1:T(8,128)S(1)} %multiply_add_fusion), dimensions={0,1,2} | broadcast | bytes 12779520 | tf_op jit(solution)/shard_map/div | solution.py:43
  182.4 12.6 %copy.15 = f32[384,2,4096]{2,0,1:T(8,128)} copy(f32[384,2,4096]{0,2,1:T(8,128)} %bitcast.10) | data formatting | bytes 25165824 | tf_op jit(solution)/shard_map/div | solution.py:43
  195.1 10.2 %divide_convert_fusion = bf16[384,2,2,4096]{3,0,2,1:T(8,128)(2,1)S(1)} fusion(f32[384,2,4096]{2,0,1:T(8,128)} %copy.15, f32[2,2,4096]{2,1,0:T(2,128)S(1)} %broadcast_multiply_fusion, bf16[128,2,2,4096]{3,0,2,1:T(8,128)(2,1)} %collective-permute-done.1, bf16[128,2,2,4096]{3,0,2,1:T(8,128)(2,1)} %copy.11, bf16[128,2,2,4096]{3,0,2,1:T(8,128)(2,1)} %collective-permute-done), kind=kLoop, calls=%fused_computation.2 | loop fusion | flops 56623104 | bytes 37814272 | tf_op jit(solution)/shard_map/convert_element_type | solution.py:46
  205.2 30.0 %copy.17 = bf16[384,2,2,4096]{3,2,1,0:T(2,128)(2,1)} copy(bf16[384,2,2,4096]{3,0,2,1:T(8,128)(2,1)S(1)} %divide_convert_fusion) | data formatting | bytes 25165824 | tf_op jit(solution)/shard_map/convert_element_type | solution.py:46
  235.2 47.0 %gather_fusion = bf16[512,2,2,4096]{3,2,1,0:T(2,128)(2,1)} fusion(bf16[384,2,2,4096]{3,2,1,0:T(2,128)(2,1)} %copy.17, s32[1024]{0:T(1024)S(1)} %pad_clamp_fusion.1), kind=kCustom, calls=%fused_computation | custom fusion | bytes 33556480 | tf_op jit(solution)/shard_map/while/body/eval_jaxpr/gather | solution.py:79
  282.2 17.6 %convert_element_type.33 = f32[512,2,2,4096]{3,2,1,0:T(2,128)} convert(bf16[512,2,2,4096]{3,2,1,0:T(2,128)(2,1)} %gather_fusion) | non-fusion elementwise | flops 8388608 | bytes 50331648 | tf_op jit(solution)/shard_map/while/body/eval_jaxpr/convert_element_type | solution.py:50
  299.8 46.8 %gather_fusion.1 = bf16[512,2,2,4096]{3,2,1,0:T(2,128)(2,1)} fusion(bf16[384,2,2,4096]{3,2,1,0:T(2,128)(2,1)} %copy.17, s32[1024]{0:T(1024)S(1)} %pad_clamp_fusion), kind=kCustom, calls=%fused_computation.1 | custom fusion | bytes 33556480 | tf_op jit(solution)/shard_map/while/body/eval_jaxpr/gather | solution.py:79
  346.6 17.6 %convert_element_type.34 = f32[512,2,2,4096]{3,2,1,0:T(2,128)} convert(bf16[512,2,2,4096]{3,2,1,0:T(2,128)(2,1)} %gather_fusion.1) | non-fusion elementwise | flops 8388608 | bytes 50331648 | tf_op jit(solution)/shard_map/while/body/eval_jaxpr/convert_element_type | solution.py:51
  364.2 0.0 copy-start
  364.2 113.5 %add_reduce_fusion = (bf16[512,4096]{1,0:T(8,128)(2,1)S(1)}, bf16[512,4096]{1,0:T(8,128)(2,1)S(1)}) fusion(f32[512,2,2,4096]{3,2,1,0:T(2,128)} %convert_element_type.34, f32[512,2,2,4096]{3,2,1,0:T(2,128)} %convert_element_type.33), kind=kLoop, calls=%fused_computation.5 | loop fusion | flops 29360128 | bytes 75497472 | tf_op jit(solution)/shard_map/while/body/eval_jaxpr/reduce_sum | solution.py:52
  477.7 0.0 copy-done
  477.8 7.6 %fusion.15 = f32[512,512]{1,0:T(8,128)} fusion(bf16[4096,512]{1,0:T(8,128)(2,1)} %get-tuple-element.28, bf16[4096,512]{1,0:T(8,128)(2,1)S(1)} %copy-done, bf16[512,4096]{1,0:T(8,128)(2,1)S(1)} %get-tuple-element.16, bf16[512,4096]{1,0:T(8,128)(2,1)S(1)} %get-tuple-element.15, f32[512]{0:T(512)S(1)} %multiply_bitcast_fusion), kind=kOutput, calls=%fused_computation.29 | convolution fusion | flops 4328783872 | bytes 17827840 | tf_op jit(solution)/shard_map/while/body/eval_jaxpr/dot_general | solution.py:80
  (7 shorter events, 0.1 us)
Async XLA Ops:
  6.5 19.2 %copy-start.1 = (s32[4,128,2]{1,2,0:T(2,128)S(1)}, s32[4,128,2]{1,2,0:T(2,128)}, u32[]{:S(2)}) copy-start(s32[4,128,2]{1,2,0:T(2,128)} %param.4) | copy-start | bytes 12292
  6.5 19.2 %copy-start.2 = (s32[4,128]{1,0:T(4,128)S(1)}, s32[4,128]{1,0:T(4,128)}, u32[]{:S(2)}) copy-start(s32[4,128]{1,0:T(4,128)} %param.5) | copy-start | bytes 6148
  6.5 136.5 %all-reduce.2.cloned.1.call-start = ((), (), s32[]{:S(2)}) async-start(), calls=%async_computation | async-start | bytes 131072 | tf_op jit(solution)/shard_map/psum | solution.py:66
  13.6 130.3 %collective-permute-start = (bf16[128,2,2,4096]{3,0,2,1:T(8,128)(2,1)}, bf16[128,2,2,4096]{3,0,2,1:T(8,128)(2,1)}, u32[]{:S(2)}, u32[]{:S(2)}) collective-permute-start(bf16[128,2,2,4096]{3,0,2,1:T(8,128)(2,1)} %copy.11), channel_id=1, source_target_pairs={{0,1},{1,2},{2,3},{3,4},{4,5},{5,6},{6,7},{7,8},{8,9},{9,10},{10,1... | collective-permute-start | bytes 12582920 | tf_op jit(solution)/shard_map/ppermute | solution.py:20
  17.3 126.6 %collective-permute-start.1 = (bf16[128,2,2,4096]{3,0,2,1:T(8,128)(2,1)}, bf16[128,2,2,4096]{3,0,2,1:T(8,128)(2,1)}, u32[]{:S(2)}, u32[]{:S(2)}) collective-permute-start(bf16[128,2,2,4096]{3,0,2,1:T(8,128)(2,1)} %copy.11), channel_id=1, source_target_pairs={{1,0},{2,1},{3,2},{4,3},{5,4},{6,5},{7,6},{8,7},{9,8},{10,9},{11,1... | collective-permute-start | bytes 12582920 | tf_op jit(solution)/shard_map/ppermute | solution.py:23
  364.2 113.5 %copy-start = (bf16[4096,512]{1,0:T(8,128)(2,1)S(1)}, bf16[4096,512]{1,0:T(8,128)(2,1)}, u32[]{:S(2)}) copy-start(bf16[4096,512]{1,0:T(8,128)(2,1)} %get-tuple-element.26) | copy-start | bytes 12582916
Sparse Core Ops, SparseCore 0:
  25.8 117.1 all-reduce.1
where the time goes:
time: 497 us; the launch traced here: 492 us
  other arithmetic  222 us (45%)
  local copies, waits for them, and re-layouts  161 us (32%)
  waiting for transfers between devices  82.1 us (17%)
  between operations  13.5 us (3%)
  matrix products  7.64 us (2%)
  starting transfers between devices  5.62 us (1%)
    reduce_sum x1, other arithmetic, cross_rows(): jnp.sum(first_f32[:, :, 0] * second_f32[:, :, 0] + first_f32[:, :, 1] * s...  114 us
    psum x1, waiting for transfers between devices, body(): common = lax.psum(local_sum, 'row') / channels  82 us
    gather x1, local copies, waits for them, and re-layouts, correlate(): band_rows[index_rows[:, 0]]  47 us
    gather x1, local copies, waits for them, and re-layouts, correlate(): band_rows[index_rows[:, 1]]  46.8 us
    another operation x1, other arithmetic  35.2 us
    convert_element_type x1, local copies, waits for them, and re-layouts, whiten(): return scaled.reshape(raw_rows.shape).astype(jnp.bfloat16)  30 us
    div x2, local copies, waits for them, and re-layouts, whiten(): removed.reshape(row_count, window_count, 2, bin_count // BAND, BAND)  17.9 us
    convert_element_type x1, other arithmetic, cross_rows(): first_f32 = first_rows.astype(jnp.float32)  17.6 us
  transfers between devices with their start and end apart: 3, of which 1 were waited for; matrix products, arithmetic and copies ran while one was open for 9% of the time, Pallas kernels for 0%

commit v1 on v0

v1 whole, which is shorter than its diff:
```python
import functools
import math

import jax
import jax.numpy as jnp
from jax import lax
from jax.experimental import pallas as pl
from jax.experimental.pallas import tpu as pltpu
from jax.sharding import PartitionSpec as P

BAND = 64
LAGS = 512
HALO = 128
CHUNK = 256


def permuted(block, axis):
    count = lax.axis_size(axis)
    forward = [(i, i + 1) for i in range(count - 1)]
    backward = [(target, source) for source, target in forward]
    low = lax.ppermute(block[block.shape[0] - HALO :], axis, forward)
    high = lax.ppermute(block[:HALO], axis, backward)
    return low, high


def phase_table(bins, bin_total):
    shifts = jnp.arange(LAGS, dtype=jnp.int32)[None, :] - LAGS // 2
    phase_int = jnp.mod(bins[:, None] * shifts, 2 * bin_total)
    angle_rad = phase_int.astype(jnp.float32) * (math.pi / bin_total)
    return jnp.cos(angle_rad), jnp.sin(angle_rad)


def kernel(windows, norm_factor, *refs):
    parts = 2 * windows
    raw = [refs[i * parts : (i + 1) * parts] for i in range(3)]
    common_ref, first_ref, second_ref, live_ref, cl_ref, sl_ref, ch_ref, sh_ref = refs[
        3 * parts : 3 * parts + 8
    ]
    out_ref, pick_a, pick_b, white = refs[3 * parts + 8 :]
    step = pl.program_id(0)
    rows, total_rows = raw[1][0].shape[0], white.shape[0]
    pairs = out_ref.shape[0]
    chunk = raw[0][0].shape[1]

    @pl.when(step == 0)
    def _():
        own = lax.broadcasted_iota(jnp.int32, (pairs, rows), 1)
        pick_a[...] = (first_ref[...] == own).astype(jnp.float32).astype(jnp.bfloat16)
        band = lax.broadcasted_iota(jnp.int32, (pairs, total_rows), 1)
        pick_b[...] = (second_ref[...] == band).astype(jnp.float32).astype(jnp.bfloat16)
        out_ref[...] = jnp.zeros_like(out_ref)

    lane_r = lax.broadcasted_iota(jnp.int32, (chunk, chunk), 0) // BAND
    lane_c = lax.broadcasted_iota(jnp.int32, (chunk, chunk), 1) // BAND
    same = (lane_r == lane_c).astype(jnp.float32).astype(jnp.bfloat16)
    start = 0
    for side in range(3):
        count = raw[side][0].shape[0]
        for w in range(windows):
            re = raw[side][2 * w][...].astype(jnp.float32) - common_ref[2 * w : 2 * w + 1, :]
            im = raw[side][2 * w + 1][...].astype(jnp.float32) - common_ref[2 * w + 1 : 2 * w + 2, :]
            mag = jnp.sqrt(re * re + im * im)
            hi = mag.astype(jnp.bfloat16)
            lo = (mag - hi.astype(jnp.float32)).astype(jnp.bfloat16)
            level = jnp.dot(hi, same, preferred_element_type=jnp.float32)
            level += jnp.dot(lo, same, preferred_element_type=jnp.float32)
            scale = 1.0 / (level * (1.0 / BAND) + 1e-06)
            at = 2 * w * chunk
            white[start : start + count, at : at + chunk] = (re * scale).astype(jnp.bfloat16)
            white[start : start + count, at + chunk : at + 2 * chunk] = (im * scale).astype(jnp.bfloat16)
        start += count

    cl, sl, ch, sh = cl_ref[...], sl_ref[...], ch_ref[0], sh_ref[0]
    lag_re = (cl * ch - sl * sh).astype(jnp.bfloat16)
    lag_im = (-(sl * ch + cl * sh)).astype(jnp.bfloat16)
    low_rows = raw[0][0].shape[0]
    tile = 128

    def one(i, carry):
        at = pl.ds(pl.multiple_of(i * tile, tile), tile)
        a = jnp.dot(pick_a[at, :], white[low_rows : low_rows + rows, :], preferred_element_type=jnp.float32)
        b = jnp.dot(pick_b[at, :], white[...], preferred_element_type=jnp.float32)
        cross_re = jnp.zeros((tile, chunk), jnp.float32)
        cross_im = jnp.zeros((tile, chunk), jnp.float32)
        for w in range(windows):
            lo = 2 * w * chunk
            ar, ai = a[:, lo : lo + chunk], a[:, lo + chunk : lo + 2 * chunk]
            br, bi = b[:, lo : lo + chunk], b[:, lo + chunk : lo + 2 * chunk]
            cross_re += ar * br + ai * bi
            cross_im += ai * br - ar * bi
        total = jnp.dot(cross_re.astype(jnp.bfloat16), lag_re, preferred_element_type=jnp.float32)
        total += jnp.dot(cross_im.astype(jnp.bfloat16), lag_im, preferred_element_type=jnp.float32)
        out_ref[at, :] += total
        return carry

    lax.fori_loop(0, pairs // tile, one, 0)

    @pl.when(step == pl.num_programs(0) - 1)
    def _():
        out_ref[...] = out_ref[...] * (norm_factor * live_ref[...])


def body(spectra, pair_channels, pair_live):
    own_rows, windows, _, bins = spectra.shape
    channels = own_rows * lax.axis_size("row")
    first_own = lax.axis_index("row") * own_rows
    flat = spectra.reshape(own_rows, windows * 2 * bins)
    low, high = permuted(flat, "row")
    local_sum = jnp.sum(spectra, axis=0, dtype=jnp.float32)
    common = (lax.psum(local_sum, "row") / channels).reshape(windows * 2, bins)
    steps = bins // CHUNK
    cl, sl = phase_table(jnp.arange(CHUNK, dtype=jnp.int32), bins)
    ch, sh = phase_table(jnp.arange(steps, dtype=jnp.int32) * CHUNK, bins)
    tile_count, tile_pairs = pair_live.shape
    pairs = tile_count * tile_pairs
    index = pair_channels.reshape(pairs, 2)
    first = index[:, 0:1] - first_own
    second = index[:, 1:2] - (first_own - HALO)
    live = pair_live.reshape(pairs, 1).astype(jnp.float32)
    parts = 2 * windows

    def strips(count):
        return [pl.BlockSpec((count, CHUNK), lambda c, k=k: (0, k * steps + c)) for k in range(parts)]

    def whole(shape):
        return pl.BlockSpec(shape, lambda c: (0, 0))

    result = pl.pallas_call(
        functools.partial(kernel, windows, 1.0 / math.sqrt(bins * windows)),
        grid=(steps,),
        out_shape=jax.ShapeDtypeStruct((pairs, LAGS), jnp.float32),
        in_specs=strips(HALO) + strips(own_rows) + strips(HALO) + [
            pl.BlockSpec((parts, CHUNK), lambda c: (0, c)),
            whole((pairs, 1)), whole((pairs, 1)), whole((pairs, 1)),
            whole((CHUNK, LAGS)), whole((CHUNK, LAGS)),
            pl.BlockSpec((1, 1, LAGS), lambda c: (c, 0, 0)),
            pl.BlockSpec((1, 1, LAGS), lambda c: (c, 0, 0)),
        ],
        out_specs=whole((pairs, LAGS)),
        scratch_shapes=[
            pltpu.VMEM((pairs, own_rows), jnp.bfloat16),
            pltpu.VMEM((pairs, own_rows + 2 * HALO), jnp.bfloat16),
            pltpu.VMEM((own_rows + 2 * HALO, parts * CHUNK), jnp.bfloat16),
        ],
    )(*([low] * parts + [flat] * parts + [high] * parts), common, first, second, live, cl, sl,
      ch[:, None, :], sh[:, None, :])
    return result.reshape(tile_count, tile_pairs, LAGS)


def solution(mesh):
    placed = (P(("day", "row"), None, None, None), P("row", None, None), P("row", None))
    return jax.shard_map(
        body, mesh=mesh, in_specs=placed, out_specs=P(("day", "row"), None, None), check_vma=False
    )
```

time: 497 us -> 213 us (0.43)
  other arithmetic: 222 us -> 12.7 us
  local copies, waits for them, and re-layouts: 161 us -> 9.5 us
  Pallas kernels: 0 us -> 56.3 us
  waiting for transfers between devices: 82.1 us -> 111 us
  matrix products: 7.64 us -> 0 us
    reduce_sum x2 -> x0, other arithmetic: 120 us -> none  [the longest x1 114 us: cross_rows(): jnp.sum(first_f32[:, :, 0] * second_f32[:, :, 0] + first_f32[:, :, 1] * s...]
    gather x2 -> x0, local copies, waits for them, and re-layouts: 93.9 us -> none  [the longest x1 47 us: correlate(): band_rows[index_rows[:, 0]]]
    pallas_call x0 -> x1, Pallas kernels: none -> 56.3 us  [body(): pl.pallas_call(functools.partial(kernel, windows, 1.0 / math.sqrt(bins *...]
    convert_element_type x3 -> x2, other arithmetic: 45.4 us -> 0.09 us  [the longest x1 0.09 us: phase_table(): angle_rad = phase_int.astype(jnp.float32) * (math.pi / bin_total)]
    another operation x1 -> x0, other arithmetic: 35.2 us -> none
    convert_element_type x1, local copies, waits for them, and re-layouts: 30 us -> 0.85 us  [body(): live = pair_live.reshape(pairs, 1).astype(jnp.float32)]
    psum x1, waiting for transfers between devices: 82 us -> 111 us  [body(): common = (lax.psum(local_sum, 'row') / channels).reshape(windows * 2, bins)]
    div x2 -> x0, local copies, waits for them, and re-layouts: 17.9 us -> none  [whiten(): removed.reshape(row_count, window_count, 2, bin_count // BAND, BAND)]
  transfers between devices with their start and end apart: 3 -> 3, of which waited for: 1 -> 1; matrix products, arithmetic and copies ran while one was open for 9% -> 7% of each run, Pallas kernels for 0% -> 0%
where the time goes in v1:
time: 213 us; the launch traced here: 209 us
  waiting for transfers between devices  111 us (52%)
  Pallas kernels  56.3 us (26%)
  between operations  13.5 us (6%)
  other arithmetic  12.7 us (6%)
  local copies, waits for them, and re-layouts  9.5 us (4%)
  starting transfers between devices  6.59 us (3%)
    psum x1, waiting for transfers between devices, body(): common = (lax.psum(local_sum, 'row') / channels).reshape(windows * 2, bins)  111 us
    pallas_call x1, Pallas kernels, body(): pl.pallas_call(functools.partial(kernel, windows, 1.0 / math.sqrt(bins *...  56.3 us
    reshape x1, local copies, waits for them, and re-layouts, body(): flat = spectra.reshape(own_rows, windows * 2 * bins)  7.81 us
    reduce_sum x1, other arithmetic, body(): local_sum = jnp.sum(spectra, axis=0, dtype=jnp.float32)  6.37 us
    sin x2, other arithmetic, phase_table(): return (jnp.cos(angle_rad), jnp.sin(angle_rad))  4.51 us
  transfers between devices with their start and end apart: 3, of which 1 were waited for; matrix products, arithmetic and copies ran while one was open for 7% of the time, Pallas kernels for 0%

profile of v1, /device:TPU:7, one launch (start us, length us, event | category | flops | bytes accessed | tf_op | source)
XLA Modules:
  0.0 209.1 jit_solution(18358618359060412724)
XLA Ops:
  6.5 0.0 all-reduce.2.cloned.1.call-start
  6.5 7.8 %reshape.155.refs_4_.refs_5_.refs_6_.refs_7_ = bf16[128,16384]{1,0:T(8,128)(2,1)} reshape(bf16[128,2,2,4096]{3,2,1,0:T(2,128)(2,1)} %param.3) | data formatting | bytes 8388608 | tf_op jit(solution)/shard_map/reshape | solution.py:107
  14.3 0.0 copy-start
  14.3 0.0 copy-start.1
  14.4 2.7 %collective-permute-start.1 = (bf16[128,16384]{1,0:T(8,128)(2,1)}, bf16[128,16384]{1,0:T(8,128)(2,1)}, u32[]{:S(2)}, u32[]{:S(2)}) collective-permute-start(bf16[128,16384]{1,0:T(8,128)(2,1)} %reshape.155.refs_4_.refs_5_.refs_6_.refs_7_), channel_id=1, source_target_pairs={{1,0},{2,1},{3,2},{4,3},{5,4},{6,5},{7,6},{8,7},{9,8},{10,9},{11,1... | collective-permute-start | bytes 12582920 | tf_op jit(solution)/shard_map/ppermute | solution.py:22
  17.1 3.9 %collective-permute-start = (bf16[128,16384]{1,0:T(8,128)(2,1)}, bf16[128,16384]{1,0:T(8,128)(2,1)}, u32[]{:S(2)}, u32[]{:S(2)}) collective-permute-start(bf16[128,16384]{1,0:T(8,128)(2,1)} %reshape.155.refs_4_.refs_5_.refs_6_.refs_7_), channel_id=1, source_target_pairs={{0,1},{1,2},{2,3},{3,4},{4,5},{5,6},{6,7},{7,8},{8,9},{9,10},{10,1... | collective-permute-start | bytes 12582920 | tf_op jit(solution)/shard_map/ppermute | solution.py:21
  20.9 6.4 %convert_reduce_fusion = f32[2,2,4096]{2,1,0:T(2,128)} fusion(bf16[128,2,2,4096]{3,2,1,0:T(2,128)(2,1)} %param.3), kind=kLoop, calls=%fused_computation | loop fusion | flops 4177920 | bytes 4259840 | tf_op jit(solution)/shard_map/reduce_sum | solution.py:109
  27.3 0.0 all-reduce.2.cloned.1.call-update
  27.4 0.0 copy-done
  27.4 0.1 copy.7
  27.5 0.1 fusion.8
  27.6 0.9 slice_subtract_fusion
  28.5 3.0 %fusion.6 = (f32[256,512]{1,0:T(8,128)}, f32[256,512]{1,0:T(8,128)}) fusion(s32[512]{0:T(512)S(1)} %iota_add_fusion), kind=kLoop, calls=%fused_computation.12 | loop fusion | flops 1835008 | bytes 1050624 | tf_op jit(solution)/shard_map/sin | solution.py:30
  31.4 1.6 fusion.10
  33.0 0.0 copy-done.1
  33.0 0.9 copy.9.refs_15_
  33.9 110.5 %all-reduce.2.cloned.1.call-done = f32[2,2,4096]{2,1,0:T(2,128)} async-done(((f32[2,2,4096]{2,1,0:T(2,128)}), f32[2,2,4096]{2,1,0:T(2,128)}) %all-reduce.2.cloned.1.call-update) | async-done | bytes 65552 | tf_op jit(solution)/shard_map/psum | solution.py:110
  144.4 0.9 broadcast_multiply_fusion
  145.3 0.7 reshape.156.refs_12_
  146.0 0.0 collective-permute-done.1.refs_8_.refs_9_.refs_10_.refs_11_
  146.0 0.0 collective-permute-done.refs_0_.refs_1_.refs_2_.refs_3_
  146.0 56.3 %shard_map.37 = f32[512,512]{1,0:T(8,128)} custom-call(bf16[128,16384]{1,0:T(8,128)(2,1)} %collective-permute-done.refs_0_.refs_1_.refs_2_.refs_3_, bf16[128,16384]{1,0:T(8,128)(2,1)} %collective-permute-done.refs_0_.refs_1_.refs_2_.refs_3_, bf16[128,16384]{1,0:T(8,128)(2,1)} %collective-permute-done.refs_0_.refs_1_.refs_2_.refs_3_, ...), custom_call_target="tpu_custom_call" | custom-call | tf_op jit(solution)/shard_map/pallas_call | solution.py:128
  (3 shorter events, 0.0 us)
Async XLA Ops:
  6.5 137.9 %all-reduce.2.cloned.1.call-start = ((), (), s32[]{:S(2)}) async-start(), calls=%async_computation | async-start | bytes 131072 | tf_op jit(solution)/shard_map/psum | solution.py:110
  14.3 13.0 %copy-start = (s32[4,128,2]{1,2,0:T(2,128)S(1)}, s32[4,128,2]{1,2,0:T(2,128)}, u32[]{:S(2)}) copy-start(s32[4,128,2]{1,2,0:T(2,128)} %param.4) | copy-start | bytes 12292
  14.3 18.7 %copy-start.1 = (s32[4,128]{1,0:T(4,128)S(1)}, s32[4,128]{1,0:T(4,128)}, u32[]{:S(2)}) copy-start(s32[4,128]{1,0:T(4,128)} %param.5) | copy-start | bytes 6148
  14.4 131.6 %collective-permute-start.1 = (bf16[128,16384]{1,0:T(8,128)(2,1)}, bf16[128,16384]{1,0:T(8,128)(2,1)}, u32[]{:S(2)}, u32[]{:S(2)}) collective-permute-start(bf16[128,16384]{1,0:T(8,128)(2,1)} %reshape.155.refs_4_.refs_5_.refs_6_.refs_7_), channel_id=1, source_target_pairs={{1,0},{2,1},{3,2},{4,3},{5,4},{6,5},{7,6},{8,7},{9,8},{10,9},{11,1... | collective-permute-start | bytes 12582920 | tf_op jit(solution)/shard_map/ppermute | solution.py:22
  17.1 128.9 %collective-permute-start = (bf16[128,16384]{1,0:T(8,128)(2,1)}, bf16[128,16384]{1,0:T(8,128)(2,1)}, u32[]{:S(2)}, u32[]{:S(2)}) collective-permute-start(bf16[128,16384]{1,0:T(8,128)(2,1)} %reshape.155.refs_4_.refs_5_.refs_6_.refs_7_), channel_id=1, source_target_pairs={{0,1},{1,2},{2,3},{3,4},{4,5},{5,6},{6,7},{7,8},{8,9},{9,10},{10,1... | collective-permute-start | bytes 12582920 | tf_op jit(solution)/shard_map/ppermute | solution.py:21
Sparse Core Ops, SparseCore 0:
  27.5 116.8 all-reduce.1

commit v2 on v1

v2 whole, which is shorter than its diff:
```python
import functools
import math

import jax
import jax.numpy as jnp
from jax import lax
from jax.experimental import pallas as pl
from jax.experimental.pallas import tpu as pltpu
from jax.sharding import PartitionSpec as P

BAND = 64
LAGS = 512
CHUNK = 256
PRE = 4


def phase_table(bins, bin_total):
    shifts = jnp.arange(LAGS, dtype=jnp.int32)[None, :] - LAGS // 2
    phase_int = jnp.mod(bins[:, None] * shifts, 2 * bin_total)
    angle_rad = phase_int.astype(jnp.float32) * (math.pi / bin_total)
    return jnp.cos(angle_rad), jnp.sin(angle_rad)


MESH = pl.DeviceIdType.MESH


def kernel(count, windows, norm_factor, own_hbm, first_ref, second_ref, live_ref, cl_ref, sl_ref, ch_ref, sh_ref,
           out_ref, own, halo, pick_a, pick_b, white, sums, heard,
           load_sem, send_sem, recv_sem, sum_send, sum_recv):
    parts = 2 * windows
    steps, rows, width = own.shape
    chunk = width // parts
    bins = steps * chunk
    pairs = out_ref.shape[0]
    me = lax.axis_index("row")
    rounds = count.bit_length() - 1
    channels = count * rows

    def load(c, k):
        return pltpu.make_async_copy(
            own_hbm.at[:, pl.ds(pl.multiple_of(k * bins + c * chunk, chunk), chunk)],
            own.at[c, :, pl.ds(k * chunk, chunk)], load_sem.at[c, k])

    def send(side, c, target):
        return pltpu.make_async_remote_copy(
            src_ref=own.at[c], dst_ref=halo.at[side, c], send_sem=send_sem.at[side, c],
            recv_sem=recv_sem.at[side, c], device_id={"row": target}, device_id_type=MESH)

    def send_chunk(c):
        @pl.when(me < count - 1)
        def _():
            send(0, c, me + 1).start()

        @pl.when(me > 0)
        def _():
            send(1, c, me - 1).start()

    for k in range(parts):
        @pl.loop(0, steps)
        def _(c, k=k):
            load(c, k).start()

    barrier = pltpu.get_barrier_semaphore()
    partners = [me ^ (1 << r) for r in range(rounds)]
    for partner in partners:
        pl.semaphore_signal(barrier, inc=1, device_id={"row": partner}, device_id_type=MESH)

    other = lax.rem(me + 2 * lax.rem(me, 2) - 1 + count, count)
    pl.semaphore_signal(barrier, inc=1, device_id={"row": other}, device_id_type=MESH)

    own_index = lax.broadcasted_iota(jnp.int32, (pairs, rows), 1)
    pick_a[...] = (first_ref[...] == own_index).astype(jnp.float32).astype(jnp.bfloat16)
    band = lax.broadcasted_iota(jnp.int32, (pairs, white.shape[0]), 1)
    pick_b[...] = (second_ref[...] == band).astype(jnp.float32).astype(jnp.bfloat16)
    out_ref[...] = jnp.zeros_like(out_ref)

    @pl.when(me == 0)
    def _():
        @pl.loop(0, steps)
        def _(c):
            halo[0, c] = jnp.zeros((rows, width), jnp.bfloat16)

    @pl.when(me == count - 1)
    def _():
        @pl.loop(0, steps)
        def _(c):
            halo[1, c] = jnp.zeros((rows, width), jnp.bfloat16)

    @pl.loop(0, steps)
    def _(c):
        for k in range(parts):
            load(c, k).wait()
            block = own[c, :, k * chunk : (k + 1) * chunk].astype(jnp.float32)
            sums[0, c, k : k + 1, :] = jnp.sum(block, axis=0, keepdims=True)

    pl.semaphore_wait(barrier, rounds + 1)

    copies = []
    for r in range(rounds):
        copy = pltpu.make_async_remote_copy(
            src_ref=sums.at[r], dst_ref=heard.at[r], send_sem=sum_send.at[r], recv_sem=sum_recv.at[r],
            device_id={"row": partners[r]}, device_id_type=MESH)
        copy.start()
        copies.append(copy)
        if r < min(PRE, steps):
            send_chunk(r)
        copy.wait_recv()
        sums[r + 1] = sums[r] + heard[r]

    @pl.loop(min(PRE, rounds, steps), steps)
    def _(c):
        send_chunk(c)

    lane_r = lax.broadcasted_iota(jnp.int32, (chunk, chunk), 0) // BAND
    lane_c = lax.broadcasted_iota(jnp.int32, (chunk, chunk), 1) // BAND
    same = (lane_r == lane_c).astype(jnp.float32).astype(jnp.bfloat16)

    def whiten(c, source, start):
        for w in range(windows):
            at = 2 * w * chunk
            common = sums[rounds, c] * (1.0 / channels)
            re = source[:, at : at + chunk].astype(jnp.float32) - common[2 * w : 2 * w + 1, :]
            im = source[:, at + chunk : at + 2 * chunk].astype(jnp.float32) - common[2 * w + 1 : 2 * w + 2, :]
            mag = jnp.sqrt(re * re + im * im)
            hi = mag.astype(jnp.bfloat16)
            lo = (mag - hi.astype(jnp.float32)).astype(jnp.bfloat16)
            level = jnp.dot(hi, same, preferred_element_type=jnp.float32)
            level += jnp.dot(lo, same, preferred_element_type=jnp.float32)
            scale = 1.0 / (level * (1.0 / BAND) + 1e-06)
            white[start : start + rows, at : at + chunk] = (re * scale).astype(jnp.bfloat16)
            white[start : start + rows, at + chunk : at + 2 * chunk] = (im * scale).astype(jnp.bfloat16)

    @pl.loop(0, steps)
    def _(c):
        whiten(c, own.at[c], rows)

        @pl.when(me > 0)
        def _():
            send(0, c, me - 1).wait_recv()

        whiten(c, halo.at[0, c], 0)

        @pl.when(me < count - 1)
        def _():
            send(1, c, me + 1).wait_recv()

        whiten(c, halo.at[1, c], 2 * rows)
        cl, sl, ch, sh = cl_ref[...], sl_ref[...], ch_ref[c], sh_ref[c]
        lag_re = (cl * ch - sl * sh).astype(jnp.bfloat16)
        lag_im = (-(sl * ch + cl * sh)).astype(jnp.bfloat16)
        tile = 128

        @pl.loop(0, pairs // tile)
        def _(i):
            at = pl.ds(pl.multiple_of(i * tile, tile), tile)
            a = jnp.dot(pick_a[at, :], white[rows : 2 * rows, :], preferred_element_type=jnp.float32)
            b = jnp.dot(pick_b[at, :], white[...], preferred_element_type=jnp.float32)
            cross_re = jnp.zeros((tile, chunk), jnp.float32)
            cross_im = jnp.zeros((tile, chunk), jnp.float32)
            for w in range(windows):
                lo = 2 * w * chunk
                ar, ai = a[:, lo : lo + chunk], a[:, lo + chunk : lo + 2 * chunk]
                br, bi = b[:, lo : lo + chunk], b[:, lo + chunk : lo + 2 * chunk]
                cross_re += ar * br + ai * bi
                cross_im += ai * br - ar * bi
            total = jnp.dot(cross_re.astype(jnp.bfloat16), lag_re, preferred_element_type=jnp.float32)
            total += jnp.dot(cross_im.astype(jnp.bfloat16), lag_im, preferred_element_type=jnp.float32)
            out_ref[at, :] += total

    out_ref[...] = out_ref[...] * (norm_factor * live_ref[...])
    for copy in copies:
        copy.wait_send()

    @pl.loop(0, steps)
    def _(c):
        @pl.when(me < count - 1)
        def _():
            send(0, c, me + 1).wait_send()

        @pl.when(me > 0)
        def _():
            send(1, c, me - 1).wait_send()


def body(spectra, pair_channels, pair_live):
    rows, windows, _, bins = spectra.shape
    count = lax.axis_size("row")
    first_own = lax.axis_index("row") * rows
    parts = 2 * windows
    flat = spectra.reshape(rows, parts * bins)
    steps = bins // CHUNK
    cl, sl = phase_table(jnp.arange(CHUNK, dtype=jnp.int32), bins)
    ch, sh = phase_table(jnp.arange(steps, dtype=jnp.int32) * CHUNK, bins)
    tile_count, tile_pairs = pair_live.shape
    pairs = tile_count * tile_pairs
    index = pair_channels.reshape(pairs, 2)
    first = index[:, 0:1] - first_own
    second = index[:, 1:2] - (first_own - rows)
    live = pair_live.reshape(pairs, 1).astype(jnp.float32)
    rounds = count.bit_length() - 1
    vmem = pl.BlockSpec(memory_space=pltpu.VMEM)
    result = pl.pallas_call(
        functools.partial(kernel, count, windows, 1.0 / math.sqrt(bins * windows)),
        out_shape=jax.ShapeDtypeStruct((pairs, LAGS), jnp.float32),
        in_specs=[pl.BlockSpec(memory_space=pl.ANY)] + [vmem] * 7,
        out_specs=vmem,
        scratch_shapes=[
            pltpu.VMEM((steps, rows, parts * CHUNK), jnp.bfloat16),
            pltpu.VMEM((2, steps, rows, parts * CHUNK), jnp.bfloat16),
            pltpu.VMEM((pairs, rows), jnp.bfloat16),
            pltpu.VMEM((pairs, 3 * rows), jnp.bfloat16),
            pltpu.VMEM((3 * rows, parts * CHUNK), jnp.bfloat16),
            pltpu.VMEM((rounds + 1, steps, parts, CHUNK), jnp.float32),
            pltpu.VMEM((rounds, steps, parts, CHUNK), jnp.float32),
            pltpu.SemaphoreType.DMA((steps, parts)),
            pltpu.SemaphoreType.DMA((2, steps)),
            pltpu.SemaphoreType.DMA((2, steps)),
            pltpu.SemaphoreType.DMA((rounds,)),
            pltpu.SemaphoreType.DMA((rounds,)),
        ],
        compiler_params=pltpu.CompilerParams(
            collective_id=0, has_side_effects=True, vmem_limit_bytes=60 * 2**20),
    )(flat, first, second, live, cl, sl, ch[:, None, :], sh[:, None, :])
    return result.reshape(tile_count, tile_pairs, LAGS)


def solution(mesh):
    placed = (P(("day", "row"), None, None, None), P("row", None, None), P("row", None))
    return jax.shard_map(
        body, mesh=mesh, in_specs=placed, out_specs=P(("day", "row"), None, None), check_vma=False
    )
```

time: 213 us -> 132 us (0.62)
  the two profiles are of different devices: /device:TPU:7 before, /device:TPU:9 now
where the time goes in v2:
time: 132 us
  Pallas kernels  114 us (86%)
  local copies, waits for them, and re-layouts  11.8 us (9%)
  other arithmetic  6.18 us (5%)
    pallas_call x1, Pallas kernels, body(): pl.pallas_call(functools.partial(kernel, count, windows, 1.0 / math.sqrt(...  114 us
    reshape x1, local copies, waits for them, and re-layouts, body(): flat = spectra.reshape(rows, parts * bins)  7.81 us
    sin x2, other arithmetic, phase_table(): return (jnp.cos(angle_rad), jnp.sin(angle_rad))  4.51 us
    unnamed x2, local copies, waits for them, and re-layouts  3.09 us

profile of v2, /device:TPU:9, one launch (start us, length us, event | category | flops | bytes accessed | tf_op | source)
XLA Modules:
  0.0 131.5 jit_solution(2960786003312273277)
XLA Ops:
  0.0 0.7 convert_element_type.26
  0.7 0.1 fusion.8
  0.8 1.6 %fusion.10 = (f32[16,1,512]{2,1,0:T(1,128)}, f32[16,1,512]{2,1,0:T(1,128)}) fusion(f32[16,1,512]{2,0,1:T(8,128)S(1)} %fusion.8), kind=kLoop, calls=%fused_computation.22 | loop fusion | flops 8192 | bytes 98304 | tf_op jit(solution)/shard_map/sin | solution.py:21
  2.4 0.9 copy.9.live_ref
  3.2 0.8 copy.7
  4.1 0.9 slice_subtract_fusion
  5.0 2.9 %fusion.6 = (f32[256,512]{1,0:T(8,128)}, f32[256,512]{1,0:T(8,128)}) fusion(s32[512]{0:T(512)S(1)} %iota_add_fusion), kind=kLoop, calls=%fused_computation.11 | loop fusion | flops 1835008 | bytes 1050624 | tf_op jit(solution)/shard_map/sin | solution.py:21
  7.9 7.8 %reshape.152.own_hbm = bf16[128,16384]{1,0:T(8,128)(2,1)} reshape(bf16[128,2,2,4096]{3,2,1,0:T(2,128)(2,1)} %param.3) | data formatting | bytes 8388608 | tf_op jit(solution)/shard_map/reshape | solution.py:190
  15.7 113.6 %shard_map.37 = f32[512,512]{1,0:T(8,128)} custom-call(bf16[128,16384]{1,0:T(8,128)(2,1)} %reshape.152.own_hbm, s32[512,1]{1,0:T(8,128)} %get-tuple-element.6.first_ref, s32[512,1]{1,0:T(8,128)} %get-tuple-element.5.second_ref, f32[512,1]{1,0:T(8,128)} %copy.9.live_ref, f32[256,512]{1,0:T(8,128)} %get-tuple-element.10.cl_ref, ...), custom_call_target="tpu_custom_call" | custom-call | tf_op jit(solution)/shard_map/pallas_call | solution.py:202
  129.3 2.3 %copy.16 = f32[4,128,512]{2,1,0:T(8,128)} copy(f32[4,128,512]{2,1,0:T(8,128)} %bitcast.3) | data formatting | bytes 2097152
  (2 shorter events, 0.0 us)

commit v3 on v2

v3 whole, which is shorter than its diff:
```python
import functools
import math

import jax
import jax.numpy as jnp
from jax import lax
from jax.experimental import pallas as pl
from jax.experimental.pallas import tpu as pltpu
from jax.sharding import PartitionSpec as P

BAND = 64
LAGS = 512
CHUNK = 256
TILE = 256


MESH = pl.DeviceIdType.MESH


def kernel(count, windows, norm_factor, own_hbm, pack_ref, out_ref, own, halo, pack, pick_a, pick_b, white,
           base, acc, back_out, back_in, sums, heard,
           load_sem, send_sem, recv_sem, sum_send, sum_recv, pack_send, pack_recv, back_send, back_recv):
    parts = 2 * windows
    steps, rows, width = own.shape
    half = steps // 2
    chunk = width // parts
    bins = steps * chunk
    pairs = out_ref.shape[0]
    me = lax.axis_index("row")
    first_own = me * rows
    rounds = count.bit_length() - 1
    channels = count * rows
    has_left, has_right = me > 0, me < count - 1

    def load(c, k):
        return pltpu.make_async_copy(
            own_hbm.at[:, pl.ds(pl.multiple_of(k * bins + c * chunk, chunk), chunk)],
            own.at[c, :, pl.ds(k * chunk, chunk)], load_sem.at[c, k])

    def remote(src, dst, sent, got, target):
        return pltpu.make_async_remote_copy(
            src_ref=src, dst_ref=dst, send_sem=sent, recv_sem=got,
            device_id={"row": target}, device_id_type=MESH)

    def send(c, target):
        return remote(own.at[c], halo.at[c], send_sem.at[c], recv_sem.at[c], target)

    def send_pack(side, target):
        return remote(pack_ref, pack.at[side], pack_send.at[side], pack_recv.at[side], target)

    def send_back(side, target):
        return remote(back_out.at[side], back_in.at[side], back_send.at[side], back_recv.at[side], target)

    for k in range(parts):
        @pl.loop(0, steps)
        def _(c, k=k):
            load(c, k).start()

    barrier = pltpu.get_barrier_semaphore()
    partners = [me ^ (1 << r) for r in range(rounds)]
    for partner in partners:
        pl.semaphore_signal(barrier, inc=1, device_id={"row": partner}, device_id_type=MESH)
    other = lax.rem(me + 2 * lax.rem(me, 2) - 1 + count, count)
    pl.semaphore_signal(barrier, inc=1, device_id={"row": other}, device_id_type=MESH)

    acc[...] = jnp.zeros_like(acc)

    @pl.when(jnp.logical_not(has_left))
    def _():
        pack[0] = jnp.zeros(pack.shape[1:], jnp.int32)

        @pl.loop(0, half)
        def _(c):
            halo[c] = jnp.zeros((rows, width), jnp.bfloat16)

    @pl.when(jnp.logical_not(has_right))
    def _():
        pack[1] = jnp.zeros(pack.shape[1:], jnp.int32)

        @pl.loop(half, steps)
        def _(c):
            halo[c] = jnp.zeros((rows, width), jnp.bfloat16)

    @pl.loop(0, steps)
    def _(c):
        for k in range(parts):
            load(c, k).wait()
            block = own[c, :, k * chunk : (k + 1) * chunk].astype(jnp.float32)
            sums[0, c, k : k + 1, :] = jnp.sum(block, axis=0, keepdims=True)

    pl.semaphore_wait(barrier, rounds + 1)

    def add_up(r):
        copy = remote(sums.at[r], heard.at[r], sum_send.at[r], sum_recv.at[r], partners[r])
        copy.start()
        return copy

    copies = [add_up(0)]

    @pl.when(has_right)
    def _():
        send_pack(0, me + 1).start()

    @pl.when(has_left)
    def _():
        send_pack(1, me - 1).start()

    for r in range(rounds):
        if r == 0:
            shifts = lax.broadcasted_iota(jnp.int32, (chunk, LAGS), 1) + (2 * bins - LAGS // 2)
            phase = lax.rem(lax.broadcasted_iota(jnp.int32, (chunk, LAGS), 0) * shifts, 2 * bins)
            angle = phase.astype(jnp.float32) * (math.pi / bins)
            base[0] = jnp.cos(angle)
            base[1] = jnp.sin(angle)
        if r == 1:
            @pl.when(has_left)
            def _():
                send_pack(0, me - 1).wait_recv()

            @pl.when(has_right)
            def _():
                send_pack(1, me + 1).wait_recv()

            row = lax.broadcasted_iota(jnp.int32, (2 * rows, pairs), 0)
            for side in range(2):
                beside = first_own - rows if side == 0 else first_own + rows

                def pick(index, near):
                    inside = (index >= first_own) & (index < first_own + rows)
                    mine = jnp.where(inside, index - first_own + rows, -1)
                    if not near:
                        return mine
                    across = (index >= beside) & (index < beside + rows)
                    return jnp.where(across, index - beside, mine)

                for group in range(2):
                    table = pack_ref[...] if group == side_own(side) else pack[side]
                    first, second, live = table[0:1], table[1:2], table[2:3].astype(jnp.float32)
                    near = group == side_own(side)
                    at = slice(group * pairs, (group + 1) * pairs)
                    a_row = pick(first, True)
                    b_row = pick(second, near)
                    hot_a = (row == a_row).astype(jnp.float32) * live
                    hot_b = (row == b_row).astype(jnp.float32)
                    pick_a[side, at, :] = jnp.transpose(hot_a).astype(jnp.bfloat16)
                    pick_b[side, at, :] = jnp.transpose(hot_b).astype(jnp.bfloat16)
        copies[r].wait_recv()
        sums[r + 1] = sums[r] + heard[r]
        if r + 1 < rounds:
            copies.append(add_up(r + 1))

    @pl.when(has_right)
    def _():
        @pl.loop(0, half)
        def _(c):
            send(c, me + 1).start()

    lane_r = lax.broadcasted_iota(jnp.int32, (chunk, chunk), 0) // BAND
    lane_c = lax.broadcasted_iota(jnp.int32, (chunk, chunk), 1) // BAND
    same = (lane_r == lane_c).astype(jnp.float32).astype(jnp.bfloat16)

    def whiten(c, source, start):
        common = sums[rounds, c] * (1.0 / channels)
        for w in range(windows):
            at = 2 * w * chunk
            re = source[:, at : at + chunk].astype(jnp.float32) - common[2 * w : 2 * w + 1, :]
            im = source[:, at + chunk : at + 2 * chunk].astype(jnp.float32) - common[2 * w + 1 : 2 * w + 2, :]
            power = re * re + im * im
            mag = power * lax.rsqrt(jnp.maximum(power, 1e-30))
            hi = mag.astype(jnp.bfloat16)
            lo = (mag - hi.astype(jnp.float32)).astype(jnp.bfloat16)
            level = jnp.dot(hi, same, preferred_element_type=jnp.float32)
            level += jnp.dot(lo, same, preferred_element_type=jnp.float32)
            scale = 1.0 / (level * (1.0 / BAND) + 1e-06)
            white[start : start + rows, at : at + chunk] = (re * scale).astype(jnp.bfloat16)
            white[start : start + rows, at + chunk : at + 2 * chunk] = (im * scale).astype(jnp.bfloat16)

    shift_row = lax.broadcasted_iota(jnp.int32, (8, LAGS), 1) + (2 * bins - LAGS // 2)

    def correlate(side, c):
        turn = lax.rem(lax.rem(c * shift_row, 2 * bins) * chunk, 2 * bins).astype(jnp.float32) * (math.pi / bins)
        ch, sh = jnp.cos(turn)[0:1], jnp.sin(turn)[0:1]
        lag_re = (base[0] * ch - base[1] * sh).astype(jnp.bfloat16)
        lag_im = (-(base[1] * ch + base[0] * sh)).astype(jnp.bfloat16)
        tile = TILE

        @pl.loop(0, 2 * pairs // tile)
        def _(i):
            at = pl.ds(pl.multiple_of(i * tile, tile), tile)
            to = pl.ds(pl.multiple_of(side * pairs + i * tile, tile), tile)
            cross_re = jnp.zeros((tile, chunk), jnp.float32)
            cross_im = jnp.zeros((tile, chunk), jnp.float32)
            for w in range(windows):
                lo = 2 * w * chunk
                a = jnp.dot(pick_a[side, at, :], white[:, lo : lo + 2 * chunk], preferred_element_type=jnp.float32)
                b = jnp.dot(pick_b[side, at, :], white[:, lo : lo + 2 * chunk], preferred_element_type=jnp.float32)
                ar, ai, br, bi = a[:, :chunk], a[:, chunk:], b[:, :chunk], b[:, chunk:]
                cross_re += ar * br + ai * bi
                cross_im += ai * br - ar * bi
            total = jnp.dot(cross_re.astype(jnp.bfloat16), lag_re, preferred_element_type=jnp.float32)
            total += jnp.dot(cross_im.astype(jnp.bfloat16), lag_im, preferred_element_type=jnp.float32)
            acc[to, :] += total

    @pl.loop(0, half)
    def _(c):
        @pl.when(has_left)
        def _():
            send(half + c, me - 1).start()

        whiten(c, own.at[c], rows)

        @pl.when(has_left)
        def _():
            send(c, me - 1).wait_recv()

        whiten(c, halo.at[c], 0)
        correlate(0, c)

    back_out[0] = acc[0:pairs, :].astype(jnp.bfloat16)

    @pl.when(has_left)
    def _():
        send_back(0, me - 1).start()

    @pl.loop(half, steps)
    def _(c):
        whiten(c, own.at[c], rows)

        @pl.when(has_right)
        def _():
            send(c, me + 1).wait_recv()

        whiten(c, halo.at[c], 0)
        correlate(1, c)

    back_out[1] = acc[2 * pairs : 3 * pairs, :].astype(jnp.bfloat16)

    @pl.when(has_right)
    def _():
        send_back(1, me + 1).start()
        send_back(0, me + 1).wait_recv()
        acc[pairs : 2 * pairs, :] += back_in[0].astype(jnp.float32)

    @pl.when(has_left)
    def _():
        send_back(1, me - 1).wait_recv()
        acc[pairs : 2 * pairs, :] += back_in[1].astype(jnp.float32)

    out_ref[...] = acc[pairs : 2 * pairs, :] * norm_factor
    for copy in copies:
        copy.wait_send()

    @pl.when(has_right)
    def _():
        send_pack(0, me + 1).wait_send()
        send_back(1, me + 1).wait_send()

        @pl.loop(0, half)
        def _(c):
            send(c, me + 1).wait_send()

    @pl.when(has_left)
    def _():
        send_pack(1, me - 1).wait_send()
        send_back(0, me - 1).wait_send()

        @pl.loop(half, steps)
        def _(c):
            send(c, me - 1).wait_send()


def side_own(side):
    return 1 - side


def body(spectra, pair_channels, pair_live):
    rows, windows, _, bins = spectra.shape
    count = lax.axis_size("row")
    parts = 2 * windows
    flat = spectra.reshape(rows, parts * bins)
    steps = bins // CHUNK
    tile_count, tile_pairs = pair_live.shape
    pairs = tile_count * tile_pairs
    index = jnp.transpose(pair_channels, (2, 0, 1)).reshape(2, pairs)
    packed = jnp.concatenate([index, pair_live.reshape(1, pairs)], axis=0)
    rounds = count.bit_length() - 1
    vmem = pl.BlockSpec(memory_space=pltpu.VMEM)
    dma = pltpu.SemaphoreType.DMA
    result = pl.pallas_call(
        functools.partial(kernel, count, windows, 1.0 / math.sqrt(bins * windows)),
        out_shape=jax.ShapeDtypeStruct((pairs, LAGS), jnp.float32),
        in_specs=[pl.BlockSpec(memory_space=pl.ANY), vmem],
        out_specs=vmem,
        scratch_shapes=[
            pltpu.VMEM((steps, rows, parts * CHUNK), jnp.bfloat16),
            pltpu.VMEM((steps, rows, parts * CHUNK), jnp.bfloat16),
            pltpu.VMEM((2, 3, pairs), jnp.int32),
            pltpu.VMEM((2, 2 * pairs, 2 * rows), jnp.bfloat16),
            pltpu.VMEM((2, 2 * pairs, 2 * rows), jnp.bfloat16),
            pltpu.VMEM((2 * rows, parts * CHUNK), jnp.bfloat16),
            pltpu.VMEM((2, CHUNK, LAGS), jnp.float32),
            pltpu.VMEM((3 * pairs, LAGS), jnp.float32),
            pltpu.VMEM((2, pairs, LAGS), jnp.bfloat16),
            pltpu.VMEM((2, pairs, LAGS), jnp.bfloat16),
            pltpu.VMEM((rounds + 1, steps, parts, CHUNK), jnp.float32),
            pltpu.VMEM((rounds, steps, parts, CHUNK), jnp.float32),
            dma((steps, parts)), dma((steps,)), dma((steps,)), dma((rounds,)), dma((rounds,)),
            dma((2,)), dma((2,)), dma((2,)), dma((2,)),
        ],
        compiler_params=pltpu.CompilerParams(
            collective_id=0, has_side_effects=True, vmem_limit_bytes=60 * 2**20),
    )(flat, packed)
    return result.reshape(tile_count, tile_pairs, LAGS)


def solution(mesh):
    placed = (P(("day", "row"), None, None, None), P("row", None, None), P("row", None))
    return jax.shard_map(
        body, mesh=mesh, in_specs=placed, out_specs=P(("day", "row"), None, None), check_vma=False
    )
```

time: 132 us -> 120 us (0.909)
  the two profiles are of different devices: /device:TPU:9 before, /device:TPU:7 now
where the time goes in v3:
time: 120 us; the launch traced here: 119 us
  Pallas kernels  108 us (90%)
  local copies, waits for them, and re-layouts  10.1 us (8%)
  other arithmetic  1.31 us (1%)
    pallas_call x1, Pallas kernels, body(): pl.pallas_call(functools.partial(kernel, count, windows, 1.0 / math.sqrt(...  108 us
    reshape x1, local copies, waits for them, and re-layouts, body(): flat = spectra.reshape(rows, parts * bins)  7.82 us

profile of v3, /device:TPU:7, one launch (start us, length us, event | category | flops | bytes accessed | tf_op | source)
XLA Modules:
  0.0 119.2 jit_solution(5439098329355911068)
XLA Ops:
  0.0 1.3 %pad_add_fusion.pack_ref = s32[3,512]{1,0:T(4,128)} fusion(s32[1,512]{1,0:T(1,128)} %bitcast.7, s32[2,512]{1,0:T(2,128)} %bitcast.6), kind=kLoop, calls=%fused_computation | loop fusion | flops 1536 | bytes 12288 | tf_op jit(solution)/shard_map/concatenate | solution.py:285
  1.3 7.8 %reshape.12.own_hbm = bf16[128,16384]{1,0:T(8,128)(2,1)} reshape(bf16[128,2,2,4096]{3,2,1,0:T(2,128)(2,1)} %param.3) | data formatting | bytes 8388608 | tf_op jit(solution)/shard_map/reshape | solution.py:280
  9.1 107.8 %shard_map.37 = f32[512,512]{1,0:T(8,128)} custom-call(bf16[128,16384]{1,0:T(8,128)(2,1)} %reshape.12.own_hbm, s32[3,512]{1,0:T(4,128)} %pad_add_fusion.pack_ref), custom_call_target="tpu_custom_call" | custom-call | tf_op jit(solution)/shard_map/pallas_call | solution.py:289
  116.9 2.3 %copy.5 = f32[4,128,512]{2,1,0:T(8,128)} copy(f32[4,128,512]{2,1,0:T(8,128)} %bitcast.5) | data formatting | bytes 2097152

commit v4 on v3

--- a/solution.py
+++ b/solution.py
@@ -11,7 +11,7 @@
 BAND = 64
 LAGS = 512
 CHUNK = 256
-TILE = 256
+TILE = 512
 
 
 MESH = pl.DeviceIdType.MESH
@@ -203,9 +203,10 @@
 
     @pl.loop(0, half)
     def _(c):
-        @pl.when(has_left)
+        @pl.when(has_left & (c >= half // 2))
         def _():
-            send(half + c, me - 1).start()
+            send(2 * c, me - 1).start()
+            send(2 * c + 1, me - 1).start()
 
         whiten(c, own.at[c], rows)
 

time: 120 us -> 112 us (0.933)
  Pallas kernels: 108 us -> 99.9 us
    pallas_call x1, Pallas kernels: 108 us -> 99.9 us  [body(): pl.pallas_call(functools.partial(kernel, count, windows, 1.0 / math.sqrt(...]
where the time goes in v4:
time: 112 us; the launch traced here: 111 us
  Pallas kernels  99.9 us (89%)
  local copies, waits for them, and re-layouts  10.1 us (9%)
  other arithmetic  1.31 us (1%)
    pallas_call x1, Pallas kernels, body(): pl.pallas_call(functools.partial(kernel, count, windows, 1.0 / math.sqrt(...  99.9 us
    reshape x1, local copies, waits for them, and re-layouts, body(): flat = spectra.reshape(rows, parts * bins)  7.82 us
    unnamed x1, local copies, waits for them, and re-layouts  2.26 us

profile of v4, /device:TPU:7, one launch (start us, length us, event | category | flops | bytes accessed | tf_op | source)
XLA Modules:
  0.0 111.3 jit_solution(4548321279220527280)
XLA Ops:
  0.0 1.3 %pad_add_fusion.pack_ref = s32[3,512]{1,0:T(4,128)} fusion(s32[1,512]{1,0:T(1,128)} %bitcast.7, s32[2,512]{1,0:T(2,128)} %bitcast.6), kind=kLoop, calls=%fused_computation | loop fusion | flops 1536 | bytes 12288 | tf_op jit(solution)/shard_map/concatenate | solution.py:286
  1.3 7.8 %reshape.12.own_hbm = bf16[128,16384]{1,0:T(8,128)(2,1)} reshape(bf16[128,2,2,4096]{3,2,1,0:T(2,128)(2,1)} %param.3) | data formatting | bytes 8388608 | tf_op jit(solution)/shard_map/reshape | solution.py:281
  9.1 99.9 %shard_map.37 = f32[512,512]{1,0:T(8,128)} custom-call(bf16[128,16384]{1,0:T(8,128)(2,1)} %reshape.12.own_hbm, s32[3,512]{1,0:T(4,128)} %pad_add_fusion.pack_ref), custom_call_target="tpu_custom_call" | custom-call | tf_op jit(solution)/shard_map/pallas_call | solution.py:290
  109.0 2.3 %copy.5 = f32[4,128,512]{2,1,0:T(8,128)} copy(f32[4,128,512]{2,1,0:T(8,128)} %bitcast.5) | data formatting | bytes 2097152

commit v5 on v4

--- a/solution.py
+++ b/solution.py
@@ -149,11 +149,15 @@
         if r + 1 < rounds:
             copies.append(add_up(r + 1))
 
-    @pl.when(has_right)
-    def _():
-        @pl.loop(0, half)
-        def _(c):
+    @pl.loop(0, half)
+    def _(c):
+        @pl.when(has_right)
+        def _():
             send(c, me + 1).start()
+
+        @pl.when(has_left)
+        def _():
+            send(half + c, me - 1).start()
 
     lane_r = lax.broadcasted_iota(jnp.int32, (chunk, chunk), 0) // BAND
     lane_c = lax.broadcasted_iota(jnp.int32, (chunk, chunk), 1) // BAND
@@ -203,11 +207,6 @@
 
     @pl.loop(0, half)
     def _(c):
-        @pl.when(has_left & (c >= half // 2))
-        def _():
-            send(2 * c, me - 1).start()
-            send(2 * c + 1, me - 1).start()
-
         whiten(c, own.at[c], rows)
 
         @pl.when(has_left)
@@ -216,23 +215,20 @@
 
         whiten(c, halo.at[c], 0)
         correlate(0, c)
-
-    back_out[0] = acc[0:pairs, :].astype(jnp.bfloat16)
-
-    @pl.when(has_left)
-    def _():
-        send_back(0, me - 1).start()
-
-    @pl.loop(half, steps)
-    def _(c):
-        whiten(c, own.at[c], rows)
+        whiten(half + c, own.at[half + c], rows)
 
         @pl.when(has_right)
         def _():
-            send(c, me + 1).wait_recv()
-
-        whiten(c, halo.at[c], 0)
-        correlate(1, c)
+            send(half + c, me + 1).wait_recv()
+
+        whiten(half + c, halo.at[half + c], 0)
+        correlate(1, half + c)
+
+    back_out[0] = acc[0:pairs, :].astype(jnp.bfloat16)
+
+    @pl.when(has_left)
+    def _():
+        send_back(0, me - 1).start()
 
     back_out[1] = acc[2 * pairs : 3 * pairs, :].astype(jnp.bfloat16)
 

time: 112 us -> 113 us (level)
  the two profiles are of different devices: /device:TPU:7 before, /device:TPU:11 now
where the time goes in v5:
time: 113 us; the launch traced here: 112 us
  Pallas kernels  101 us (89%)
  local copies, waits for them, and re-layouts  10.1 us (9%)
  other arithmetic  1.31 us (1%)
    pallas_call x1, Pallas kernels, body(): pl.pallas_call(functools.partial(kernel, count, windows, 1.0 / math.sqrt(...  101 us
    reshape x1, local copies, waits for them, and re-layouts, body(): flat = spectra.reshape(rows, parts * bins)  7.82 us
    unnamed x1, local copies, waits for them, and re-layouts  2.26 us

profile of v5, /device:TPU:11, one launch (start us, length us, event | category | flops | bytes accessed | tf_op | source)
XLA Modules:
  0.0 112.3 jit_solution(9519739614901681933)
XLA Ops:
  0.0 1.3 %pad_add_fusion.pack_ref = s32[3,512]{1,0:T(4,128)} fusion(s32[1,512]{1,0:T(1,128)} %bitcast.7, s32[2,512]{1,0:T(2,128)} %bitcast.6), kind=kLoop, calls=%fused_computation | loop fusion | flops 1536 | bytes 12288 | tf_op jit(solution)/shard_map/concatenate | solution.py:282
  1.3 7.8 %reshape.12.own_hbm = bf16[128,16384]{1,0:T(8,128)(2,1)} reshape(bf16[128,2,2,4096]{3,2,1,0:T(2,128)(2,1)} %param.3) | data formatting | bytes 8388608 | tf_op jit(solution)/shard_map/reshape | solution.py:277
  9.1 100.9 %shard_map.37 = f32[512,512]{1,0:T(8,128)} custom-call(bf16[128,16384]{1,0:T(8,128)(2,1)} %reshape.12.own_hbm, s32[3,512]{1,0:T(4,128)} %pad_add_fusion.pack_ref), custom_call_target="tpu_custom_call" | custom-call | tf_op jit(solution)/shard_map/pallas_call | solution.py:286
  110.1 2.3 %copy.5 = f32[4,128,512]{2,1,0:T(8,128)} copy(f32[4,128,512]{2,1,0:T(8,128)} %bitcast.5) | data formatting | bytes 2097152
